TPU v7x, 32 devices: a whole 2x2x4 slice. The times are simulated.
32 devices in a mesh: rep: 4 (over y, x), shard: 8 (over z, core).
Axes of the slice: x: 2, y: 2, z: 4, core: 2. Of those that a mesh axis runs over, the one named last changes fastest.
Arguments:
- tokens: bfloat16 [4096, 768], P(('rep', 'shard')), may hold values from -6 to 6
- segment_ids: int32 [32, 128], P(('rep', 'shard')), may hold values from 0 to 3, never falling along the last dimension, each value on 1 to 64 neighbouring positions
- first_gain: bfloat16 [768], P('shard'), may hold values from 0.5 to 1.5
- first_shift: bfloat16 [768], P('shard'), may hold values from -3 to 3
- qkv_weight: bfloat16 [768, 2304], P('shard'), may hold values from -3 to 3, as said below
- qv_bias: bfloat16 [2, 768], P(None, 'shard'), may hold values from -3 to 3
- proj_weight: bfloat16 [768, 768], P('shard'), may hold values from -0.625 to 0.625
- proj_bias: bfloat16 [768], P('shard'), may hold values from -3 to 3
- second_gain: bfloat16 [768], P('shard'), may hold values from 0.5 to 1.5
- second_shift: bfloat16 [768], P('shard'), may hold values from -3 to 3
- fc_weight: bfloat16 [768, 3072], P('shard'), may hold values from -0.21875 to 0.21875
- fc_bias: bfloat16 [3072], P('shard'), may hold values from -3 to 3
- out_weight: bfloat16 [3072, 768], P('shard'), may hold values from -0.109375 to 0.109375
- out_bias: bfloat16 [768], P('shard'), may hold values from -3 to 3
- cotangent: bfloat16 [4096, 768], P(('rep', 'shard')), may hold values from -6 to 6
Outputs:
- block_output: bfloat16 [4096, 768], P(('rep', 'shard'))
- grad_tokens: float32 [4096, 768], P(('rep', 'shard'))
- grad_first_gain: float32 [768], P('shard')
- grad_first_shift: float32 [768], P('shard')
- grad_qkv_weight: float32 [768, 2304], P('shard')
- grad_qv_bias: float32 [2, 768], P(None, 'shard')
- grad_proj_weight: float32 [768, 768], P('shard')
- grad_proj_bias: float32 [768], P('shard')
- grad_second_gain: float32 [768], P('shard')
- grad_second_shift: float32 [768], P('shard')
- grad_fc_weight: float32 [768, 3072], P('shard')
- grad_fc_bias: float32 [3072], P('shard')
- grad_out_weight: float32 [3072, 768], P('shard')
- grad_out_bias: float32 [768], P('shard')
Inputs may be any that keep to these rules, and one draw needn't show every extreme that they name: `segment_ids`: each row holds 4 runs of equal numbers in rising order, each run 1 to 64 long, one of them exactly 64. `qkv_weight`: columns 0 to 767 project to queries, the next 768 columns to keys, the last 768 columns to values.
All inputs are finite; a program needn't handle non-finite values.
Results may differ from a plain program's by a relative error of at most 0.011.
Values may be sent and summed in bfloat16 or wider, within the bound.
A program may use at most 128 MiB of HBM per device.

v0:
```python
import math
import jax
import jax.numpy as jnp
from jax import lax
from jax.sharding import PartitionSpec as P

D = 768
HEADS = 12
HD = 64
FF = 3072
EPSILON = 1e-05


def layer_norm(field, norm_gain, norm_shift):
    center = field - jnp.mean(field, axis=-1, keepdims=True)
    spread = jnp.mean(center * center, axis=-1, keepdims=True)
    return center * lax.rsqrt(spread + EPSILON) * norm_gain + norm_shift


def gelu_tanh(field):
    return jax.nn.gelu(field, approximate=True)


def head_split(matrix):
    return matrix.reshape(matrix.shape[0], HEADS, HD)


def masked_scores(query, keys, segments):
    rows = query.shape[0]
    scores = jnp.einsum(
        "qhd,khd->hqk", head_split(query), head_split(keys), preferred_element_type=jnp.float32
    ) * (1.0 / math.sqrt(HD))
    position = lax.iota(jnp.int32, rows)
    allowed = (segments[:, None] == segments[None, :]) & (position[None, :] <= position[:, None])
    return jnp.where(allowed[None], scores, -1e30)


def attend_forward(query, keys, values, segments):
    rows = query.shape[0]
    scores = masked_scores(query, keys, segments)
    row_max = jnp.max(scores, axis=-1, keepdims=True)
    row_total = jnp.sum(jnp.exp(scores - row_max), axis=-1, keepdims=True)
    logsum = row_max + jnp.log(row_total)
    probs = jnp.exp(scores - logsum).astype(jnp.bfloat16)
    attended = jnp.einsum(
        "hqk,khd->qhd", probs, head_split(values), preferred_element_type=jnp.float32
    )
    return (attended.reshape(rows, D).astype(jnp.bfloat16), logsum)


def attend_backward(query, keys, values, segments, attended, logsum, grad_attended):
    rows = query.shape[0]
    scores = masked_scores(query, keys, segments)
    weights = jnp.exp(scores - logsum)
    grad_heads = head_split(grad_attended)
    grad_values = jnp.einsum(
        "hqk,qhd->khd", weights.astype(jnp.bfloat16), grad_heads, preferred_element_type=jnp.float32
    )
    grad_probs = jnp.einsum(
        "qhd,khd->hqk", grad_heads, head_split(values), preferred_element_type=jnp.float32
    )
    delta = jnp.einsum(
        "qhd,qhd->hq", grad_heads, head_split(attended), preferred_element_type=jnp.float32
    )
    grad_scores = (weights * (grad_probs - delta[..., None]) * (1.0 / math.sqrt(HD))).astype(
        jnp.bfloat16
    )
    grad_query = jnp.einsum(
        "hqk,khd->qhd", grad_scores, head_split(keys), preferred_element_type=jnp.float32
    )
    grad_keys = jnp.einsum(
        "hqk,qhd->khd", grad_scores, head_split(query), preferred_element_type=jnp.float32
    )
    return (grad_query.reshape(rows, D), grad_keys.reshape(rows, D), grad_values.reshape(rows, D))


def exchange(field, axis, split, concat):
    return lax.all_to_all(field, axis, split_axis=split, concat_axis=concat, tiled=True)


def spread(field, axis):
    parts = lax.axis_size(axis)
    return exchange(jnp.broadcast_to(field[None], (parts,) + field.shape), axis, 0, 0)


def by_replica(field, shards, reps):
    rows = field.shape[0]
    return field.reshape(shards, reps, rows // (shards * reps), -1).swapaxes(0, 1).reshape(rows, -1)


def per_device(
    tokens,
    segment_ids,
    first_gain,
    first_shift,
    qkv_weight,
    qv_bias,
    proj_weight,
    proj_bias,
    second_gain,
    second_shift,
    fc_weight,
    fc_bias,
    out_weight,
    out_bias,
    cotangent,
):
    low = jnp.bfloat16
    segments = segment_ids[0]
    own_rows = tokens.shape[0]
    shards = lax.axis_size("shard")
    reps = lax.axis_size("rep")
    factor = 1.0 / math.sqrt(own_rows * reps * shards)
    small = jnp.stack(
        [
            first_gain,
            first_shift,
            qv_bias[0],
            qv_bias[1],
            proj_bias,
            second_gain,
            second_shift,
            out_bias,
        ]
    )
    small_full = lax.all_gather(small, "shard", axis=1, tiled=True).astype(jnp.float32)
    gain_one, shift_one, q_bias, v_bias, proj_bias_full, gain_two, shift_two, out_bias_full = (
        small_full[i] for i in range(8)
    )
    qkv_full = lax.all_gather(qkv_weight, "shard", axis=0, tiled=True)
    proj_full = lax.all_gather(proj_weight, "shard", axis=0, tiled=True)
    fc_cols = exchange(fc_weight, "shard", 1, 0)
    inputs = tokens.astype(jnp.float32)
    normed_f, first_back = jax.vjp(layer_norm, inputs, gain_one, shift_one)
    normed_first = normed_f.astype(low)
    projected = jnp.dot(normed_first, qkv_full, preferred_element_type=jnp.float32)
    query = (projected[:, :D] + q_bias).astype(low)
    keys = projected[:, D : 2 * D].astype(low)
    values = (projected[:, 2 * D :] + v_bias).astype(low)
    attended, logsum = attend_forward(query, keys, values, segments)
    residual = (
        inputs + jnp.dot(attended, proj_full, preferred_element_type=jnp.float32) + proj_bias_full
    )
    cot_f = cotangent.astype(jnp.float32)
    normed_s, second_back = jax.vjp(layer_norm, residual, gain_two, shift_two)
    normed_all = lax.all_gather(normed_s.astype(low), "shard", axis=0, tiled=True)
    cot_later, normed_all = lax.optimization_barrier((cotangent, normed_all))
    cot_all = lax.all_gather(cot_later, "shard", axis=0, tiled=True)
    pre_act = jnp.dot(normed_all, fc_cols, preferred_element_type=jnp.float32) + fc_bias.astype(
        jnp.float32
    )
    activated, gelu_back = jax.vjp(gelu_tanh, pre_act)
    hidden = activated.astype(low)
    grad_hidden = jnp.dot(cot_all, out_weight.T, preferred_element_type=jnp.float32)
    (grad_pre,) = gelu_back(grad_hidden)
    grad_pre_low = grad_pre.astype(low)
    grad_normed_part = jnp.dot(grad_pre_low, fc_cols.T, preferred_element_type=jnp.float32).astype(
        low
    )
    grad_normed_low = lax.psum_scatter(grad_normed_part, "shard", scatter_dimension=0, tiled=True)
    term_out_weight = jnp.dot(hidden.T, cot_all, preferred_element_type=jnp.float32) * factor
    term_fc_weight = (
        jnp.dot(normed_all.T, grad_pre_low, preferred_element_type=jnp.float32) * factor
    )
    out_part = jnp.dot(hidden, out_weight, preferred_element_type=jnp.float32).astype(low)
    ff_terms = jnp.concatenate(
        [
            term_out_weight.astype(low).reshape(reps, -1, D),
            by_replica(term_fc_weight.astype(low), shards, reps).reshape(reps, -1, D),
        ],
        axis=1,
    )
    ff_sum = jnp.sum(exchange(ff_terms, "rep", 0, 0).astype(jnp.float32), axis=0).astype(low)
    first_later, attended_later, grad_normed_low, ff_sum = lax.optimization_barrier(
        (normed_first, attended, grad_normed_low, ff_sum)
    )
    first_all = lax.all_gather(first_later, "shard", axis=0, tiled=True)
    grad_normed_second = grad_normed_low.astype(jnp.float32)
    grad_from_norm, second_gain_sum, second_shift_sum = second_back(grad_normed_second)
    grad_residual = cot_f + grad_from_norm
    grad_residual_low = grad_residual.astype(low)
    grad_residual_all = lax.all_gather(grad_residual_low, "shard", axis=0, tiled=True)
    attended_cols = exchange(attended_later, "shard", 1, 0)
    grad_attended = jnp.dot(
        grad_residual_low, proj_full.T, preferred_element_type=jnp.float32
    ).astype(low)
    out_rows = out_weight.shape[0] // reps
    out_piece = ff_sum[:out_rows]
    fc_piece = ff_sum[out_rows:].reshape(D // reps, -1)
    fc_piece = exchange(fc_piece, "shard", 0, 1)
    ff_all = spread(jnp.concatenate([out_piece, fc_piece.reshape(-1, D)]), "rep").astype(
        jnp.float32
    )
    grad_query, grad_keys, grad_values = attend_backward(
        query, keys, values, segments, attended, logsum, grad_attended
    )
    grad_projected = jnp.concatenate([grad_query, grad_keys, grad_values], axis=1).astype(low)
    grad_projected, ff_all = lax.optimization_barrier((grad_projected, ff_all))
    out_grad = ff_all[:, :out_rows].reshape(-1, D)
    fc_grad = ff_all[:, out_rows:].reshape(-1, FF)
    grad_cols = exchange(grad_projected, "shard", 1, 0)
    grad_normed_first = jnp.dot(grad_projected, qkv_full.T, preferred_element_type=jnp.float32)
    out_later, grad_cols = lax.optimization_barrier((out_part, grad_cols))
    out_sum = lax.psum_scatter(out_later, "shard", scatter_dimension=0, tiled=True)
    result = (residual + out_sum.astype(jnp.float32) + out_bias_full).astype(low)
    term_qkv_weight = jnp.dot(first_all.T, grad_cols, preferred_element_type=jnp.float32) * factor
    term_proj_weight = (
        jnp.dot(attended_cols.T, grad_residual_all, preferred_element_type=jnp.float32) * factor
    )
    attn_terms = jnp.concatenate(
        [
            term_proj_weight.astype(low).reshape(reps, -1, D),
            by_replica(term_qkv_weight.astype(low), shards, reps).reshape(reps, -1, D),
        ],
        axis=1,
    )
    attn_sum = jnp.sum(exchange(attn_terms, "rep", 0, 0).astype(jnp.float32), axis=0).astype(low)
    proj_rows = proj_weight.shape[0] // reps
    proj_piece = attn_sum[:proj_rows]
    qkv_piece = attn_sum[proj_rows:].reshape(D // reps, -1)
    qkv_piece = exchange(qkv_piece, "shard", 0, 1)
    attn_all = spread(jnp.concatenate([proj_piece, qkv_piece.reshape(-1, D)]), "rep").astype(
        jnp.float32
    )
    proj_grad = attn_all[:, :proj_rows].reshape(-1, D)
    qkv_grad = attn_all[:, proj_rows:].reshape(-1, 3 * D)
    grad_input_norm, first_gain_sum, first_shift_sum = first_back(grad_normed_first)
    grad_inputs = grad_residual + grad_input_norm
    terms = jnp.stack(
        [
            first_gain_sum,
            first_shift_sum,
            jnp.sum(grad_query, axis=0),
            jnp.sum(grad_values, axis=0),
            jnp.sum(grad_residual, axis=0),
            second_gain_sum,
            second_shift_sum,
            jnp.sum(cot_f, axis=0),
        ]
    )
    count = terms.shape[0]
    terms = terms.reshape(count, shards, -1).swapaxes(0, 1).reshape(shards, -1)
    own_terms = jnp.concatenate(
        [jnp.sum(exchange(terms, "shard", 0, 0), axis=0), jnp.sum(grad_pre, axis=0)]
    )
    sums = jnp.sum(spread(own_terms, "rep"), axis=0) * factor
    own_cols = D // shards
    fc_bias_grad = sums[count * own_cols :]
    sums = sums[: count * own_cols].reshape(count, own_cols)
    return (
        result,
        grad_inputs,
        sums[0],
        sums[1],
        qkv_grad,
        sums[2:4],
        proj_grad,
        sums[4],
        sums[5],
        sums[6],
        fc_grad,
        fc_bias_grad,
        out_grad,
        sums[7],
    )


def solution(mesh):
    return jax.shard_map(
        per_device,
        mesh=mesh,
        in_specs=(
            P(("rep", "shard"), None),
            P(("rep", "shard"), None),
            P("shard"),
            P("shard"),
            P("shard", None),
            P(None, "shard"),
            P("shard", None),
            P("shard"),
            P("shard"),
            P("shard"),
            P("shard", None),
            P("shard"),
            P("shard", None),
            P("shard"),
            P(("rep", "shard"), None),
        ),
        out_specs=(
            P(("rep", "shard"), None),
            P(("rep", "shard"), None),
            P("shard"),
            P("shard"),
            P("shard", None),
            P(None, "shard"),
            P("shard", None),
            P("shard"),
            P("shard"),
            P("shard"),
            P("shard", None),
            P("shard"),
            P("shard", None),
            P("shard"),
        ),
        check_vma=False,
    )
```

profile of v0, /device:TPU:0, one launch (start us, length us, event | category | flops | bytes accessed | tf_op | source)
XLA Modules:
  0.0 345.6 jit_solution(11735301634824392414)
XLA Ops:
  11.7 14.5 %all-gather = bf16[8,96,8]{1,2,0:T(8,128)(2,1)S(1)} all-gather(bf16[1,96,8]{1,2,0:T(8,128)(2,1)S(1)} %bitcast.133), channel_id=1, replica_groups=mesh['rep'=4,'shard'=8] {'shard'}, dimensions={0}, use_global_device_ids=true | all-gather | bytes 13824 | tf_op jit(solution)/shard_map/all_gather | solution.py:126
  28.9 25.1 %all-gather.8.cloned.1.call-done = bf16[768,2304]{1,0:T(8,128)(2,1)} async-done(((bf16[96,2304]{1,0:T(8,128)(2,1)}), bf16[768,2304]{1,0:T(8,128)(2,1)}) %all-gather.8.cloned.1.call-update) | async-done | bytes 3538960 | tf_op jit(solution)/shard_map/all_gather | solution.py:130
  58.0 19.2 %all-gather.10.cloned.1.call-done = bf16[768,768]{1,0:T(8,128)(2,1)} async-done(((bf16[96,768]{1,0:T(8,128)(2,1)}), bf16[768,768]{1,0:T(8,128)(2,1)}) %all-gather.10.cloned.1.call-update) | async-done | bytes 1179664 | tf_op jit(solution)/shard_map/all_gather | solution.py:131
  80.6 24.9 %all-gather.12.cloned.1.call-done = bf16[1024,768]{1,0:T(8,128)(2,1)} async-done(((bf16[128,768]{1,0:T(8,128)(2,1)}), bf16[1024,768]{1,0:T(8,128)(2,1)}) %all-gather.12.cloned.1.call-update) | async-done | bytes 1572880 | tf_op jit(solution)/shard_map/all_gather | solution.py:146
  106.4 3.5 %all-to-all-start = ((bf16[96,8,384]{2,0,1:T(8,128)(2,1)}), bf16[96,8,384]{2,0,1:T(8,128)(2,1)S(1)}, u32[]{:S(2)}, u32[]{:S(2)}) async-start(bf16[96,8,384]{2,0,1:T(8,128)(2,1)} %bitcast.106), calls=%async_computation | async-start | bytes 1179648 | tf_op jit(solution)/shard_map/all_to_all | solution.py:78
  110.0 30.8 %all-gather.14.cloned.1.call-done = bf16[1024,768]{1,0:T(8,128)(2,1)} async-done(((bf16[128,768]{1,0:T(8,128)(2,1)}), bf16[1024,768]{1,0:T(8,128)(2,1)}) %all-gather.14.cloned.1.call-update) | async-done | bytes 1572880 | tf_op jit(solution)/shard_map/all_gather | solution.py:148
  140.8 3.6 %fusion.58 = f32[1024,384]{1,0:T(8,128)} fusion(bf16[1024,768]{1,0:T(8,128)(2,1)} %all-gather.14.cloned.1.call-done, bf16[384,768]{1,0:T(8,128)(2,1)S(1)} %copy-done), kind=kOutput, calls=%fused_computation.119 | convolution fusion | flops 603979776 | bytes 3735552 | tf_op jit(solution)/shard_map/dot_general | solution.py:154
  144.4 5.6 %fusion.47 = (f32[384]{0:T(512)}, bf16[1024,384]{1,0:T(8,128)(2,1)S(1)}, f32[1024,384]{1,0:T(8,128)}) fusion(f32[1024,384]{1,0:T(8,128)} %fusion.58, f32[384]{0:T(512)S(1)} %convert_element_type.103, bf16[1024,768]{1,0:T(8,128)(2,1)} %all-gather.12.cloned.1.call-done, bf16[768,384]{1,0:T(8,128)(2,1)S(1)} %bitcast.125), kind=kOutput, calls=%fused_computation.109 | convolution fusion | flops 612630144 | bytes 6097920 | tf_op jit(solution)/shard_map/dot_general | solution.py:149
  158.9 19.4 %all_to_all.125 = bf16[4,192,768]{2,1,0:T(8,128)(2,1)S(1)} all-to-all(bf16[4,192,768]{2,1,0:T(8,128)(2,1)S(1)} %pad_maximum_fusion), channel_id=1, replica_groups=mesh['rep'=4,'shard'=8] {'rep'}, dimensions={0} | all-to-all | bytes 2359296 | tf_op jit(solution)/shard_map/all_to_all | solution.py:78
  179.2 7.8 %reduce-scatter.3.cloned.1.call-done = bf16[128,768]{1,0:T(8,128)(2,1)} async-done(((bf16[1024,768]{1,0:T(8,128)(2,1)}), bf16[128,768]{1,0:T(8,128)(2,1)}) %reduce-scatter.3.cloned.1.call-update) | async-done | bytes 196624 | tf_op jit(solution)/shard_map/reduce_scatter | solution.py:160
  190.5 4.0 %all-to-all-start.2 = ((bf16[8,24,384]{2,1,0:T(8,128)(2,1)}), bf16[8,24,384]{2,1,0:T(8,128)(2,1)}, u32[]{:S(2)}, u32[]{:S(2)}) async-start(bf16[8,24,384]{2,1,0:T(8,128)(2,1)} %all_to_all.93), calls=%async_computation.3 | async-start | bytes 294912 | tf_op jit(solution)/shard_map/all_to_all | solution.py:78
  207.6 4.6 %all-to-all-start.3 = ((bf16[4,192,768]{2,1,0:T(8,128)(2,1)}), bf16[4,192,768]{2,1,0:T(8,128)(2,1)}, u32[]{:S(2)}, u32[]{:S(2)}) async-start(bf16[4,192,768]{2,1,0:T(8,128)(2,1)} %broadcast_in_dim.34), calls=%async_computation.4 | async-start | bytes 2359296 | tf_op jit(solution)/shard_map/all_to_all | solution.py:78
  215.4 11.7 %all-to-all-done.3 = bf16[4,192,768]{2,1,0:T(8,128)(2,1)} async-done(((bf16[4,192,768]{2,1,0:T(8,128)(2,1)}), bf16[4,192,768]{2,1,0:T(8,128)(2,1)}, u32[]{:S(2)}, u32[]{:S(2)}) %all-to-all-start.3) | async-done | bytes 1179680 | tf_op jit(solution)/shard_map/all_to_all | solution.py:78
  228.6 4.2 %all-to-all-start.4 = ((bf16[128,8,288]{0,2,1:T(8,128)(2,1)}), bf16[128,8,288]{0,2,1:T(8,128)(2,1)}, u32[]{:S(2)}, u32[]{:S(2)}) async-start(bf16[128,8,288]{0,2,1:T(8,128)(2,1)} %bitcast.107), calls=%async_computation.5 | async-start | bytes 1179648 | tf_op jit(solution)/shard_map/all_to_all | solution.py:78
  232.8 3.8 %convolution_convert_fusion.1 = bf16[1024,768]{1,0:T(8,128)(2,1)} fusion(bf16[384,768]{1,0:T(8,128)(2,1)S(1)} %copy-done, f32[1024,384]{1,0:T(8,128)} %get-tuple-element.76), kind=kOutput, calls=%fused_computation.3 | convolution fusion | flops 608305152 | bytes 3735552 | tf_op jit(solution)/shard_map/dot_general | solution.py:165
  240.7 12.3 %all-to-all-done.4 = bf16[128,8,288]{0,2,1:T(8,128)(2,1)} async-done(((bf16[128,8,288]{0,2,1:T(8,128)(2,1)}), bf16[128,8,288]{0,2,1:T(8,128)(2,1)}, u32[]{:S(2)}, u32[]{:S(2)}) %all-to-all-start.4) | async-done | bytes 589856 | tf_op jit(solution)/shard_map/all_to_all | solution.py:78
  253.0 4.2 %all-to-all-start.7 = ((bf16[128,8,96]{0,2,1:T(8,128)(2,1)}), bf16[128,8,96]{0,2,1:T(8,128)(2,1)}, u32[]{:S(2)}, u32[]{:S(2)}) async-start(bf16[128,8,96]{0,2,1:T(8,128)(2,1)} %bitcast.109), calls=%async_computation.9 | async-start | bytes 393216 | tf_op jit(solution)/shard_map/all_to_all | solution.py:78
  259.3 4.2 %fusion.46 = (f32[768]{0:T(1024)}, f32[128]{0:T(128)S(1)}, f32[128,768]{1,0:T(8,128)S(1)}) fusion(f32[768]{0:T(1024)S(1)} %get-tuple-element.50, f32[128]{0:T(128)S(1)} %copy-done.20, bf16[128,768]{1,0:T(8,128)(2,1)S(1)} %copy-done.1, bf16[128,2304]{0,1:T(8,128)(2,1)} %pad_maximum_fusion.1, bf16[768,2304]{1,0:T(8,128)(2,1)} %all-gather.8.cloned.1.call-done), kind=kOutput, calls=%fused_computation.108 | convolution fusion | flops 453573760 | bytes 4725760 | tf_op jit(solution)/shard_map/dot_general | solution.py:202
  277.1 5.0 %all-to-all-start.5 = ((f32[8,1,768]{2,1,0:T(1,128)}), f32[8,1,768]{2,1,0:T(1,128)S(1)}, u32[]{:S(2)}, u32[]{:S(2)}) async-start(f32[8,1,768]{2,1,0:T(1,128)} %all_to_all.113), calls=%async_computation.7 | async-start | bytes 49152 | tf_op jit(solution)/shard_map/all_to_all | solution.py:78
  288.0 4.2 %all-to-all-start.8 = ((bf16[4,96,768]{2,1,0:T(8,128)(2,1)}), bf16[4,96,768]{2,1,0:T(8,128)(2,1)}, u32[]{:S(2)}, u32[]{:S(2)}) async-start(bf16[4,96,768]{2,1,0:T(8,128)(2,1)} %pad_maximum_fusion.2), calls=%async_computation.10 | async-start | bytes 1179648 | tf_op jit(solution)/shard_map/all_to_all | solution.py:78
  292.3 9.2 %all-to-all-done.8 = bf16[4,96,768]{2,1,0:T(8,128)(2,1)} async-done(((bf16[4,96,768]{2,1,0:T(8,128)(2,1)}), bf16[4,96,768]{2,1,0:T(8,128)(2,1)}, u32[]{:S(2)}, u32[]{:S(2)}) %all-to-all-start.8) | async-done | bytes 589856 | tf_op jit(solution)/shard_map/all_to_all | solution.py:78
  310.0 4.0 %all-to-all-start.9 = ((bf16[8,24,288]{2,1,0:T(8,128)(2,1)}), bf16[8,24,288]{2,1,0:T(8,128)(2,1)}, u32[]{:S(2)}, u32[]{:S(2)}) async-start(bf16[8,24,288]{2,1,0:T(8,128)(2,1)} %all_to_all.109), calls=%async_computation.11 | async-start | bytes 294912 | tf_op jit(solution)/shard_map/all_to_all | solution.py:78
  323.1 3.5 %all-to-all-start.10 = ((bf16[4,96,768]{2,1,0:T(8,128)(2,1)}), bf16[4,96,768]{2,1,0:T(8,128)(2,1)S(1)}, u32[]{:S(2)}, u32[]{:S(2)}) async-start(bf16[4,96,768]{2,1,0:T(8,128)(2,1)} %broadcast_in_dim.68), calls=%async_computation.12 | async-start | bytes 1179648 | tf_op jit(solution)/shard_map/all_to_all | solution.py:78
  328.5 6.6 %all-to-all-done.10 = bf16[4,96,768]{2,1,0:T(8,128)(2,1)S(1)} async-done(((bf16[4,96,768]{2,1,0:T(8,128)(2,1)}), bf16[4,96,768]{2,1,0:T(8,128)(2,1)S(1)}, u32[]{:S(2)}, u32[]{:S(2)}) %all-to-all-start.10) | async-done | bytes 589856 | tf_op jit(solution)/shard_map/all_to_all | solution.py:78
  (192 shorter events, 94.9 us)
Async XLA Ops:
  7.2 133.6 %copy-start = (bf16[384,768]{1,0:T(8,128)(2,1)S(1)}, bf16[384,768]{1,0:T(8,128)(2,1)}, u32[]{:S(2)}) copy-start(bf16[384,768]{1,0:T(8,128)(2,1)} %param.27) | copy-start | bytes 1769476
  7.2 46.7 %all-gather.8.cloned.1.call-start = ((), (), s32[]{:S(2)}) async-start(), calls=%async_computation.13 | async-start | bytes 3981312 | tf_op jit(solution)/shard_map/all_gather | solution.py:130
  7.9 69.2 %all-gather.10.cloned.1.call-start = ((), (), s32[]{:S(2)}) async-start(), calls=%async_computation.14 | async-start | bytes 1327104 | tf_op jit(solution)/shard_map/all_gather | solution.py:131
  8.7 96.8 %all-gather.12.cloned.1.call-start = ((), (), s32[]{:S(2)}) async-start(), calls=%async_computation.15 | async-start | bytes 1769472 | tf_op jit(solution)/shard_map/all_gather | solution.py:146
  9.8 46.8 %copy-start.19 = (f32[128]{0:T(128)}, f32[128]{0:T(128)S(1)}, u32[]{:S(2)}) copy-start(f32[128]{0:T(128)S(1)} %broadcast_multiply_fusion.2) | copy-start | bytes 1540
  10.9 45.7 %copy-start.23 = (f32[128]{0:T(128)}, f32[128]{0:T(128)S(1)}, u32[]{:S(2)}) copy-start(f32[128]{0:T(128)S(1)} %fusion.41) | copy-start | bytes 1540
  58.0 145.1 %copy-start.5 = (bf16[12,64,128]{2,1,0:T(8,128)(2,1)}, bf16[12,64,128]{2,1,0:T(8,128)(2,1)S(1)}, u32[]{:S(2)}) copy-start(bf16[12,64,128]{2,1,0:T(8,128)(2,1)S(1)} %convolution_convert_fusion.4) | copy-start | bytes 589828
  77.2 28.4 %copy-start.14 = (bf16[96,3072]{1,0:T(8,128)(2,1)S(1)}, bf16[96,3072]{1,0:T(8,128)(2,1)}, u32[]{:S(2)}) copy-start(bf16[96,3072]{1,0:T(8,128)(2,1)} %param.25) | copy-start | bytes 1769476
  79.7 30.3 %copy-start.29 = (bf16[384]{0:T(512)(128)(2,1)S(1)}, bf16[384]{0:T(512)(128)(2,1)}, u32[]{:S(2)}) copy-start(bf16[384]{0:T(512)(128)(2,1)} %param.26) | copy-start | bytes 2308
  80.5 60.3 %all-gather.14.cloned.1.call-start = ((), (), s32[]{:S(2)}) async-start(), calls=%async_computation.16 | async-start | bytes 1769472 | tf_op jit(solution)/shard_map/all_gather | solution.py:148
  106.4 38.0 %all-to-all-start = ((bf16[96,8,384]{2,0,1:T(8,128)(2,1)}), bf16[96,8,384]{2,0,1:T(8,128)(2,1)S(1)}, u32[]{:S(2)}, u32[]{:S(2)}) async-start(bf16[96,8,384]{2,0,1:T(8,128)(2,1)} %bitcast.106), calls=%async_computation | async-start | bytes 1179648 | tf_op jit(solution)/shard_map/all_to_all | solution.py:78
  110.0 77.1 %reduce-scatter.3.cloned.1.call-start = ((), (), s32[]{:S(2)}) async-start(), calls=%async_computation.17 | async-start | bytes 1769472 | tf_op jit(solution)/shard_map/reduce_scatter | solution.py:160
  153.1 114.3 %all-gather.18.cloned.1.call-start = ((), (), s32[]{:S(2)}) async-start(), calls=%async_computation.20 | async-start | bytes 1769472 | tf_op jit(solution)/shard_map/all_gather | solution.py:177
  190.5 14.9 %all-to-all-start.2 = ((bf16[8,24,384]{2,1,0:T(8,128)(2,1)}), bf16[8,24,384]{2,1,0:T(8,128)(2,1)}, u32[]{:S(2)}, u32[]{:S(2)}) async-start(bf16[8,24,384]{2,1,0:T(8,128)(2,1)} %all_to_all.93), calls=%async_computation.3 | async-start | bytes 294912 | tf_op jit(solution)/shard_map/all_to_all | solution.py:78
  194.5 87.6 %all-gather.16.cloned.1.call-start = ((), (), s32[]{:S(2)}) async-start(), calls=%async_computation.19 | async-start | bytes 1769472 | tf_op jit(solution)/shard_map/all_gather | solution.py:182
  207.6 19.6 %all-to-all-start.3 = ((bf16[4,192,768]{2,1,0:T(8,128)(2,1)}), bf16[4,192,768]{2,1,0:T(8,128)(2,1)}, u32[]{:S(2)}, u32[]{:S(2)}) async-start(bf16[4,192,768]{2,1,0:T(8,128)(2,1)} %broadcast_in_dim.34), calls=%async_computation.4 | async-start | bytes 2359296 | tf_op jit(solution)/shard_map/all_to_all | solution.py:78
  228.6 24.4 %all-to-all-start.4 = ((bf16[128,8,288]{0,2,1:T(8,128)(2,1)}), bf16[128,8,288]{0,2,1:T(8,128)(2,1)}, u32[]{:S(2)}, u32[]{:S(2)}) async-start(bf16[128,8,288]{0,2,1:T(8,128)(2,1)} %bitcast.107), calls=%async_computation.5 | async-start | bytes 1179648 | tf_op jit(solution)/shard_map/all_to_all | solution.py:78
  253.0 24.1 %all-to-all-start.7 = ((bf16[128,8,96]{0,2,1:T(8,128)(2,1)}), bf16[128,8,96]{0,2,1:T(8,128)(2,1)}, u32[]{:S(2)}, u32[]{:S(2)}) async-start(bf16[128,8,96]{0,2,1:T(8,128)(2,1)} %bitcast.109), calls=%async_computation.9 | async-start | bytes 393216 | tf_op jit(solution)/shard_map/all_to_all | solution.py:78
  257.1 79.9 %reduce-scatter.5.cloned.1.call-start = ((), (), s32[]{:S(2)}) async-start(), calls=%async_computation.18 | async-start | bytes 1769472 | tf_op jit(solution)/shard_map/reduce_scatter | solution.py:204
  277.1 10.9 %all-to-all-start.5 = ((f32[8,1,768]{2,1,0:T(1,128)}), f32[8,1,768]{2,1,0:T(1,128)S(1)}, u32[]{:S(2)}, u32[]{:S(2)}) async-start(f32[8,1,768]{2,1,0:T(1,128)} %all_to_all.113), calls=%async_computation.7 | async-start | bytes 49152 | tf_op jit(solution)/shard_map/all_to_all | solution.py:78
  288.0 13.4 %all-to-all-start.8 = ((bf16[4,96,768]{2,1,0:T(8,128)(2,1)}), bf16[4,96,768]{2,1,0:T(8,128)(2,1)}, u32[]{:S(2)}, u32[]{:S(2)}) async-start(bf16[4,96,768]{2,1,0:T(8,128)(2,1)} %pad_maximum_fusion.2), calls=%async_computation.10 | async-start | bytes 1179648 | tf_op jit(solution)/shard_map/all_to_all | solution.py:78
  302.1 7.9 %all-to-all-start.6 = ((f32[4,1,1152]{2,1,0:T(1,128)}), f32[4,1,1152]{2,1,0:T(1,128)S(1)}, u32[]{:S(2)}, u32[]{:S(2)}) async-start(f32[4,1,1152]{2,1,0:T(1,128)} %broadcast_in_dim.37), calls=%async_computation.8 | async-start | bytes 36864 | tf_op jit(solution)/shard_map/all_to_all | solution.py:78
  310.0 11.0 %all-to-all-start.9 = ((bf16[8,24,288]{2,1,0:T(8,128)(2,1)}), bf16[8,24,288]{2,1,0:T(8,128)(2,1)}, u32[]{:S(2)}, u32[]{:S(2)}) async-start(bf16[8,24,288]{2,1,0:T(8,128)(2,1)} %all_to_all.109), calls=%async_computation.11 | async-start | bytes 294912 | tf_op jit(solution)/shard_map/all_to_all | solution.py:78
  323.1 12.0 %all-to-all-start.10 = ((bf16[4,96,768]{2,1,0:T(8,128)(2,1)}), bf16[4,96,768]{2,1,0:T(8,128)(2,1)S(1)}, u32[]{:S(2)}, u32[]{:S(2)}) async-start(bf16[4,96,768]{2,1,0:T(8,128)(2,1)} %broadcast_in_dim.68), calls=%async_computation.12 | async-start | bytes 1179648 | tf_op jit(solution)/shard_map/all_to_all | solution.py:78
  (28 other events, 196.3 us)
Sparse Core Ops, SparseCore 0:
  9.7 44.2 all-gather.7
  55.6 21.5 all-gather.9
  80.6 24.8 all-gather.11
  107.0 33.7 all-gather.13
  153.2 33.8 reduce-scatter.2
  188.6 26.5 all-gather.17
  217.4 27.5 all-gather.15
  260.3 35.7 reduce-scatter.4
where the time goes:
time: 347 us; the launch traced here: 346 us
  waiting for transfers between devices  158 us (46%)
  starting transfers between devices  40.7 us (12%)
  local copies, waits for them, and re-layouts  40.4 us (12%)
  matrix products  39.6 us (11%)
  blocking collectives  33.9 us (10%)
  other arithmetic  18.2 us (5%)
  between operations  14.9 us (4%)
    all_to_all x10, waiting for transfers between devices, exchange(): lax.all_to_all(field, axis, split_axis=split, concat_axis=concat, tiled=T...  48.6 us
    all_to_all x10, starting transfers between devices, exchange(): lax.all_to_all(field, axis, split_axis=split, concat_axis=concat, tiled=T...  40.4 us
    all_gather x1, waiting for transfers between devices, per_device(): cot_all = lax.all_gather(cot_later, 'shard', axis=0, tiled=True)  30.8 us
    all_gather x1, waiting for transfers between devices, per_device(): qkv_full = lax.all_gather(qkv_weight, 'shard', axis=0, tiled=True)  25.1 us
    all_gather x1, waiting for transfers between devices, per_device(): lax.all_gather(normed_s.astype(low), 'shard', axis=0, tiled=True)  24.9 us
    all_to_all x1, blocking collectives, exchange(): lax.all_to_all(field, axis, split_axis=split, concat_axis=concat, tiled=T...  19.4 us
    all_gather x1, waiting for transfers between devices, per_device(): proj_full = lax.all_gather(proj_weight, 'shard', axis=0, tiled=True)  19.2 us
    all_gather x1, blocking collectives, per_device(): lax.all_gather(small, 'shard', axis=1, tiled=True).astype(jnp.float32)  14.5 us
  transfers between devices with their start and end apart: 18, of which 13 were waited for; matrix products, arithmetic and copies ran while one was open for 23% of the time, Pallas kernels for 0%

commit v1 on v0

--- a/solution.py
+++ b/solution.py
@@ -9,6 +9,17 @@
 HD = 64
 FF = 3072
 EPSILON = 1e-05
+
+
+def gather_by_hops(x, axis, d):
+    size = lax.axis_size(axis)
+    route = [(i, (i + 1) % size) for i in range(size)]
+    parts = [x]
+    for reach in range(1, size):
+        parts = [lax.ppermute(parts[0], axis, route), *parts]
+    whole = jnp.concatenate(parts, axis=d)
+    shift = (lax.axis_index(axis) + 1) * parts[-1].shape[d]
+    return jnp.roll(whole, shift, axis=d)
 
 
 def layer_norm(field, norm_gain, norm_shift):
@@ -128,7 +139,7 @@
         small_full[i] for i in range(8)
     )
     qkv_full = lax.all_gather(qkv_weight, "shard", axis=0, tiled=True)
-    proj_full = lax.all_gather(proj_weight, "shard", axis=0, tiled=True)
+    proj_full = gather_by_hops(proj_weight, "shard", 0)
     fc_cols = exchange(fc_weight, "shard", 1, 0)
     inputs = tokens.astype(jnp.float32)
     normed_f, first_back = jax.vjp(layer_norm, inputs, gain_one, shift_one)

time: 347 us -> 354 us (1.020)
  local copies, waits for them, and re-layouts: 40.4 us -> 47.8 us
    ppermute x0 -> x7, waiting for transfers between devices: none -> 40.9 us  [gather_by_hops(): parts = [lax.ppermute(parts[0], axis, route), *parts]]
    all_gather x1, waiting for transfers between devices: 25.1 us -> 0.01 us  [per_device(): qkv_full = lax.all_gather(qkv_weight, 'shard', axis=0, tiled=True)]
    all_gather x1 -> x0, waiting for transfers between devices: 19.2 us -> none  [per_device(): proj_full = lax.all_gather(proj_weight, 'shard', axis=0, tiled=True)]
    unnamed x68 -> x91, local copies, waits for them, and re-layouts: 2.26 us -> 12.5 us
  transfers between devices with their start and end apart: 18 -> 24, of which waited for: 13 -> 17; matrix products, arithmetic and copies ran while one was open for 23% -> 23% of each run, Pallas kernels for 0% -> 0%
where the time goes in v1:
time: 354 us; the launch traced here: 352 us
  waiting for transfers between devices  156 us (44%)
  local copies, waits for them, and re-layouts  47.8 us (14%)
  starting transfers between devices  41.6 us (12%)
  matrix products  39.4 us (11%)
  blocking collectives  36.5 us (10%)
  other arithmetic  16 us (5%)
  between operations  14.9 us (4%)
    all_to_all x10, waiting for transfers between devices, exchange(): lax.all_to_all(field, axis, split_axis=split, concat_axis=concat, tiled=T...  52.1 us
    ppermute x7, waiting for transfers between devices, gather_by_hops(): parts = [lax.ppermute(parts[0], axis, route), *parts]  40.9 us
    all_to_all x10, starting transfers between devices, exchange(): lax.all_to_all(field, axis, split_axis=split, concat_axis=concat, tiled=T...  40.4 us
    all_gather x1, waiting for transfers between devices, per_device(): cot_all = lax.all_gather(cot_later, 'shard', axis=0, tiled=True)  30.8 us
    all_gather x1, waiting for transfers between devices, per_device(): lax.all_gather(normed_s.astype(low), 'shard', axis=0, tiled=True)  23.6 us
    all_to_all x1, blocking collectives, exchange(): lax.all_to_all(field, axis, split_axis=split, concat_axis=concat, tiled=T...  19.4 us
    all_gather x1, blocking collectives, per_device(): lax.all_gather(small, 'shard', axis=1, tiled=True).astype(jnp.float32)  17.1 us
    unnamed x91, local copies, waits for them, and re-layouts  12.5 us
  transfers between devices with their start and end apart: 24, of which 17 were waited for; matrix products, arithmetic and copies ran while one was open for 23% of the time, Pallas kernels for 0%

profile of v1, /device:TPU:0, one launch (start us, length us, event | category | flops | bytes accessed | tf_op | source)
XLA Modules:
  0.0 352.2 jit_solution(7122555303852812721)
XLA Ops:
  8.5 7.1 %collective-permute-done = bf16[96,768]{1,0:T(8,128)(2,1)S(1)} collective-permute-done((bf16[96,768]{1,0:T(8,128)(2,1)}, bf16[96,768]{1,0:T(8,128)(2,1)S(1)}, u32[]{:S(2)}, u32[]{:S(2)}) %collective-permute-start) | collective-permute-done | bytes 147488 | tf_op jit(solution)/shard_map/ppermute | solution.py:19
  15.6 6.4 %collective-permute-done.1 = bf16[96,768]{1,0:T(8,128)(2,1)S(1)} collective-permute-done((bf16[96,768]{1,0:T(8,128)(2,1)S(1)}, bf16[96,768]{1,0:T(8,128)(2,1)S(1)}, u32[]{:S(2)}, u32[]{:S(2)}) %collective-permute-start.1) | collective-permute-done | bytes 147488 | tf_op jit(solution)/shard_map/ppermute | solution.py:19
  23.0 8.5 %collective-permute-done.2 = bf16[96,768]{1,0:T(8,128)(2,1)S(1)} collective-permute-done((bf16[96,768]{1,0:T(8,128)(2,1)S(1)}, bf16[96,768]{1,0:T(8,128)(2,1)S(1)}, u32[]{:S(2)}, u32[]{:S(2)}) %collective-permute-start.2) | collective-permute-done | bytes 147488 | tf_op jit(solution)/shard_map/ppermute | solution.py:19
  32.6 8.4 %collective-permute-done.3 = bf16[96,768]{1,0:T(8,128)(2,1)S(1)} collective-permute-done((bf16[96,768]{1,0:T(8,128)(2,1)S(1)}, bf16[96,768]{1,0:T(8,128)(2,1)S(1)}, u32[]{:S(2)}, u32[]{:S(2)}) %collective-permute-start.3) | collective-permute-done | bytes 147488 | tf_op jit(solution)/shard_map/ppermute | solution.py:19
  41.8 17.1 %all-gather = bf16[8,96,8]{1,2,0:T(8,128)(2,1)S(1)} all-gather(bf16[1,96,8]{1,2,0:T(8,128)(2,1)S(1)} %bitcast.132), channel_id=1, replica_groups=mesh['rep'=4,'shard'=8] {'shard'}, dimensions={0}, use_global_device_ids=true | all-gather | bytes 13824 | tf_op jit(solution)/shard_map/all_gather | solution.py:137
  60.9 5.0 %collective-permute-done.5 = bf16[96,768]{1,0:T(8,128)(2,1)S(1)} collective-permute-done((bf16[96,768]{1,0:T(8,128)(2,1)S(1)}, bf16[96,768]{1,0:T(8,128)(2,1)S(1)}, u32[]{:S(2)}, u32[]{:S(2)}) %collective-permute-start.5) | collective-permute-done | bytes 147488 | tf_op jit(solution)/shard_map/ppermute | solution.py:19
  66.8 5.5 %collective-permute-done.6 = bf16[96,768]{1,0:T(8,128)(2,1)S(1)} collective-permute-done((bf16[96,768]{1,0:T(8,128)(2,1)S(1)}, bf16[96,768]{1,0:T(8,128)(2,1)S(1)}, u32[]{:S(2)}, u32[]{:S(2)}) %collective-permute-start.6) | collective-permute-done | bytes 147488 | tf_op jit(solution)/shard_map/ppermute | solution.py:19
  90.8 23.6 %all-gather.9.cloned.1.call-done = bf16[1024,768]{1,0:T(8,128)(2,1)} async-done(((bf16[128,768]{1,0:T(8,128)(2,1)}), bf16[1024,768]{1,0:T(8,128)(2,1)}) %all-gather.9.cloned.1.call-update) | async-done | bytes 1572880 | tf_op jit(solution)/shard_map/all_gather | solution.py:157
  119.0 30.8 %all-gather.11.cloned.1.call-done = bf16[1024,768]{1,0:T(8,128)(2,1)} async-done(((bf16[128,768]{1,0:T(8,128)(2,1)}), bf16[1024,768]{1,0:T(8,128)(2,1)}) %all-gather.11.cloned.1.call-update) | async-done | bytes 1572880 | tf_op jit(solution)/shard_map/all_gather | solution.py:159
  153.3 5.5 %fusion.51 = (f32[384]{0:T(512)}, bf16[1024,384]{1,0:T(8,128)(2,1)S(1)}, f32[1024,384]{1,0:T(8,128)}) fusion(f32[1024,384]{1,0:T(8,128)} %fusion.62, f32[384]{0:T(512)S(1)} %convert_element_type.103, bf16[1024,768]{1,0:T(8,128)(2,1)} %all-gather.9.cloned.1.call-done, bf16[768,384]{1,0:T(8,128)(2,1)S(1)} %bitcast.123), kind=kOutput, calls=%fused_computation.129 | convolution fusion | flops 612630144 | bytes 6097920 | tf_op jit(solution)/shard_map/dot_general | solution.py:160
  167.7 19.4 %all_to_all.125 = bf16[4,192,768]{2,1,0:T(8,128)(2,1)S(1)} all-to-all(bf16[4,192,768]{2,1,0:T(8,128)(2,1)S(1)} %pad_maximum_fusion), channel_id=1, replica_groups=mesh['rep'=4,'shard'=8] {'rep'}, dimensions={0} | all-to-all | bytes 2359296 | tf_op jit(solution)/shard_map/all_to_all | solution.py:89
  188.1 7.8 %reduce-scatter.3.cloned.1.call-done = bf16[128,768]{1,0:T(8,128)(2,1)} async-done(((bf16[1024,768]{1,0:T(8,128)(2,1)}), bf16[128,768]{1,0:T(8,128)(2,1)}) %reduce-scatter.3.cloned.1.call-update) | async-done | bytes 196624 | tf_op jit(solution)/shard_map/reduce_scatter | solution.py:171
  211.4 4.4 %all-to-all-start.3 = ((bf16[4,192,768]{2,1,0:T(8,128)(2,1)}), bf16[4,192,768]{2,1,0:T(8,128)(2,1)}, u32[]{:S(2)}, u32[]{:S(2)}) async-start(bf16[4,192,768]{2,1,0:T(8,128)(2,1)} %broadcast_in_dim.34), calls=%async_computation.4 | async-start | bytes 2359296 | tf_op jit(solution)/shard_map/all_to_all | solution.py:89
  219.1 10.9 %all-to-all-done.3 = bf16[4,192,768]{2,1,0:T(8,128)(2,1)} async-done(((bf16[4,192,768]{2,1,0:T(8,128)(2,1)}), bf16[4,192,768]{2,1,0:T(8,128)(2,1)}, u32[]{:S(2)}, u32[]{:S(2)}) %all-to-all-start.3) | async-done | bytes 1179680 | tf_op jit(solution)/shard_map/all_to_all | solution.py:89
  231.6 5.1 %all-to-all-start.4 = ((bf16[128,8,288]{0,2,1:T(8,128)(2,1)}), bf16[128,8,288]{0,2,1:T(8,128)(2,1)}, u32[]{:S(2)}, u32[]{:S(2)}) async-start(bf16[128,8,288]{0,2,1:T(8,128)(2,1)} %bitcast.105), calls=%async_computation.5 | async-start | bytes 1179648 | tf_op jit(solution)/shard_map/all_to_all | solution.py:89
  236.7 3.8 %convolution_convert_fusion.1 = bf16[1024,768]{1,0:T(8,128)(2,1)} fusion(bf16[384,768]{1,0:T(8,128)(2,1)S(1)} %copy-done, f32[1024,384]{1,0:T(8,128)} %get-tuple-element.76), kind=kOutput, calls=%fused_computation.3 | convolution fusion | flops 608305152 | bytes 3735552 | tf_op jit(solution)/shard_map/dot_general | solution.py:176
  244.6 15.0 %all-to-all-done.4 = bf16[128,8,288]{0,2,1:T(8,128)(2,1)} async-done(((bf16[128,8,288]{0,2,1:T(8,128)(2,1)}), bf16[128,8,288]{0,2,1:T(8,128)(2,1)}, u32[]{:S(2)}, u32[]{:S(2)}) %all-to-all-start.4) | async-done | bytes 589856 | tf_op jit(solution)/shard_map/all_to_all | solution.py:89
  259.6 4.1 %all-to-all-start.7 = ((bf16[128,8,96]{0,2,1:T(8,128)(2,1)}), bf16[128,8,96]{0,2,1:T(8,128)(2,1)}, u32[]{:S(2)}, u32[]{:S(2)}) async-start(bf16[128,8,96]{0,2,1:T(8,128)(2,1)} %bitcast.107), calls=%async_computation.9 | async-start | bytes 393216 | tf_op jit(solution)/shard_map/all_to_all | solution.py:89
  265.9 4.2 %fusion.50 = (f32[768]{0:T(1024)}, f32[128]{0:T(128)S(1)}, f32[128,768]{1,0:T(8,128)S(1)}) fusion(f32[768]{0:T(1024)S(1)} %get-tuple-element.50, f32[128]{0:T(128)S(1)} %copy-done.21, bf16[128,768]{1,0:T(8,128)(2,1)S(1)} %copy-done.1, bf16[128,2304]{0,1:T(8,128)(2,1)} %pad_maximum_fusion.1, bf16[768,2304]{1,0:T(8,128)(2,1)} %all-gather.7.cloned.1.call-done), kind=kOutput, calls=%fused_computation.128 | convolution fusion | flops 453573760 | bytes 4725760 | tf_op jit(solution)/shard_map/dot_general | solution.py:213
  283.7 5.0 %all-to-all-start.5 = ((f32[8,1,768]{2,1,0:T(1,128)}), f32[8,1,768]{2,1,0:T(1,128)S(1)}, u32[]{:S(2)}, u32[]{:S(2)}) async-start(f32[8,1,768]{2,1,0:T(1,128)} %all_to_all.113), calls=%async_computation.7 | async-start | bytes 49152 | tf_op jit(solution)/shard_map/all_to_all | solution.py:89
  294.6 4.2 %all-to-all-start.8 = ((bf16[4,96,768]{2,1,0:T(8,128)(2,1)}), bf16[4,96,768]{2,1,0:T(8,128)(2,1)}, u32[]{:S(2)}, u32[]{:S(2)}) async-start(bf16[4,96,768]{2,1,0:T(8,128)(2,1)} %pad_maximum_fusion.2), calls=%async_computation.10 | async-start | bytes 1179648 | tf_op jit(solution)/shard_map/all_to_all | solution.py:89
  298.9 9.2 %all-to-all-done.8 = bf16[4,96,768]{2,1,0:T(8,128)(2,1)} async-done(((bf16[4,96,768]{2,1,0:T(8,128)(2,1)}), bf16[4,96,768]{2,1,0:T(8,128)(2,1)}, u32[]{:S(2)}, u32[]{:S(2)}) %all-to-all-start.8) | async-done | bytes 589856 | tf_op jit(solution)/shard_map/all_to_all | solution.py:89
  316.6 4.0 %all-to-all-start.9 = ((bf16[8,24,288]{2,1,0:T(8,128)(2,1)}), bf16[8,24,288]{2,1,0:T(8,128)(2,1)}, u32[]{:S(2)}, u32[]{:S(2)}) async-start(bf16[8,24,288]{2,1,0:T(8,128)(2,1)} %all_to_all.109), calls=%async_computation.11 | async-start | bytes 294912 | tf_op jit(solution)/shard_map/all_to_all | solution.py:89
  335.1 6.6 %all-to-all-done.10 = bf16[4,96,768]{2,1,0:T(8,128)(2,1)S(1)} async-done(((bf16[4,96,768]{2,1,0:T(8,128)(2,1)}), bf16[4,96,768]{2,1,0:T(8,128)(2,1)S(1)}, u32[]{:S(2)}, u32[]{:S(2)}) %all-to-all-start.10) | async-done | bytes 589856 | tf_op jit(solution)/shard_map/all_to_all | solution.py:89
  (227 shorter events, 115.7 us)
Async XLA Ops:
  7.2 75.9 %all-gather.7.cloned.1.call-start = ((), (), s32[]{:S(2)}) async-start(), calls=%async_computation.13 | async-start | bytes 3981312 | tf_op jit(solution)/shard_map/all_gather | solution.py:141
  7.9 106.5 %all-gather.9.cloned.1.call-start = ((), (), s32[]{:S(2)}) async-start(), calls=%async_computation.14 | async-start | bytes 1769472 | tf_op jit(solution)/shard_map/all_gather | solution.py:157
  8.0 7.6 %collective-permute-start = (bf16[96,768]{1,0:T(8,128)(2,1)}, bf16[96,768]{1,0:T(8,128)(2,1)S(1)}, u32[]{:S(2)}, u32[]{:S(2)}) collective-permute-start(bf16[96,768]{1,0:T(8,128)(2,1)} %param.21), channel_id=1, source_target_pairs={{0,1},{1,2},{2,3},{3,4},{4,5},{5,6},{6,7},{7,0},{8,9},{9,10},{10,1... | collective-permute-start | bytes 442376 | tf_op jit(solution)/shard_map/ppermute | solution.py:19
  15.6 6.4 %collective-permute-start.1 = (bf16[96,768]{1,0:T(8,128)(2,1)S(1)}, bf16[96,768]{1,0:T(8,128)(2,1)S(1)}, u32[]{:S(2)}, u32[]{:S(2)}) collective-permute-start(bf16[96,768]{1,0:T(8,128)(2,1)S(1)} %collective-permute-done), channel_id=1, source_target_pairs={{0,1},{1,2},{2,3},{3,4},{4,5},{5,6},{6,7},{7,0},{8,9},{9,10},{10,1... | collective-permute-start | bytes 442376 | tf_op jit(solution)/shard_map/ppermute | solution.py:19
  21.9 9.5 %collective-permute-start.2 = (bf16[96,768]{1,0:T(8,128)(2,1)S(1)}, bf16[96,768]{1,0:T(8,128)(2,1)S(1)}, u32[]{:S(2)}, u32[]{:S(2)}) collective-permute-start(bf16[96,768]{1,0:T(8,128)(2,1)S(1)} %collective-permute-done.1), channel_id=1, source_target_pairs={{0,1},{1,2},{2,3},{3,4},{4,5},{5,6},{6,7},{7,0},{8,9},{9,10},{10,1... | collective-permute-start | bytes 442376 | tf_op jit(solution)/shard_map/ppermute | solution.py:19
  31.4 9.5 %collective-permute-start.3 = (bf16[96,768]{1,0:T(8,128)(2,1)S(1)}, bf16[96,768]{1,0:T(8,128)(2,1)S(1)}, u32[]{:S(2)}, u32[]{:S(2)}) collective-permute-start(bf16[96,768]{1,0:T(8,128)(2,1)S(1)} %collective-permute-done.2), channel_id=1, source_target_pairs={{0,1},{1,2},{2,3},{3,4},{4,5},{5,6},{6,7},{7,0},{8,9},{9,10},{10,1... | collective-permute-start | bytes 442376 | tf_op jit(solution)/shard_map/ppermute | solution.py:19
  41.0 18.6 %collective-permute-start.4 = (bf16[96,768]{1,0:T(8,128)(2,1)S(1)}, bf16[96,768]{1,0:T(8,128)(2,1)S(1)}, u32[]{:S(2)}, u32[]{:S(2)}) collective-permute-start(bf16[96,768]{1,0:T(8,128)(2,1)S(1)} %collective-permute-done.3), channel_id=1, source_target_pairs={{0,1},{1,2},{2,3},{3,4},{4,5},{5,6},{6,7},{7,0},{8,9},{9,10},{10,1... | collective-permute-start | bytes 442376 | tf_op jit(solution)/shard_map/ppermute | solution.py:19
  59.6 6.4 %collective-permute-start.5 = (bf16[96,768]{1,0:T(8,128)(2,1)S(1)}, bf16[96,768]{1,0:T(8,128)(2,1)S(1)}, u32[]{:S(2)}, u32[]{:S(2)}) collective-permute-start(bf16[96,768]{1,0:T(8,128)(2,1)S(1)} %collective-permute-done.4), channel_id=1, source_target_pairs={{0,1},{1,2},{2,3},{3,4},{4,5},{5,6},{6,7},{7,0},{8,9},{9,10},{10,1... | collective-permute-start | bytes 442376 | tf_op jit(solution)/shard_map/ppermute | solution.py:19
  66.0 6.4 %collective-permute-start.6 = (bf16[96,768]{1,0:T(8,128)(2,1)S(1)}, bf16[96,768]{1,0:T(8,128)(2,1)S(1)}, u32[]{:S(2)}, u32[]{:S(2)}) collective-permute-start(bf16[96,768]{1,0:T(8,128)(2,1)S(1)} %collective-permute-done.5), channel_id=1, source_target_pairs={{0,1},{1,2},{2,3},{3,4},{4,5},{5,6},{6,7},{7,0},{8,9},{9,10},{10,1... | collective-permute-start | bytes 442376 | tf_op jit(solution)/shard_map/ppermute | solution.py:19
  90.7 59.0 %all-gather.11.cloned.1.call-start = ((), (), s32[]{:S(2)}) async-start(), calls=%async_computation.15 | async-start | bytes 1769472 | tf_op jit(solution)/shard_map/all_gather | solution.py:159
  115.3 38.0 %all-to-all-start = ((bf16[96,8,384]{2,0,1:T(8,128)(2,1)}), bf16[96,8,384]{2,0,1:T(8,128)(2,1)S(1)}, u32[]{:S(2)}, u32[]{:S(2)}) async-start(bf16[96,8,384]{2,0,1:T(8,128)(2,1)} %bitcast.104), calls=%async_computation | async-start | bytes 1179648 | tf_op jit(solution)/shard_map/all_to_all | solution.py:89
  118.9 77.0 %reduce-scatter.3.cloned.1.call-start = ((), (), s32[]{:S(2)}) async-start(), calls=%async_computation.16 | async-start | bytes 1769472 | tf_op jit(solution)/shard_map/reduce_scatter | solution.py:171
  161.9 112.1 %all-gather.15.cloned.1.call-start = ((), (), s32[]{:S(2)}) async-start(), calls=%async_computation.19 | async-start | bytes 1769472 | tf_op jit(solution)/shard_map/all_gather | solution.py:188
  197.7 12.6 %all-to-all-start.2 = ((bf16[8,24,384]{2,1,0:T(8,128)(2,1)}), bf16[8,24,384]{2,1,0:T(8,128)(2,1)S(1)}, u32[]{:S(2)}, u32[]{:S(2)}) async-start(bf16[8,24,384]{2,1,0:T(8,128)(2,1)} %all_to_all.93), calls=%async_computation.3 | async-start | bytes 294912 | tf_op jit(solution)/shard_map/all_to_all | solution.py:89
  201.0 87.7 %all-gather.13.cloned.1.call-start = ((), (), s32[]{:S(2)}) async-start(), calls=%async_computation.18 | async-start | bytes 1769472 | tf_op jit(solution)/shard_map/all_gather | solution.py:193
  211.4 18.6 %all-to-all-start.3 = ((bf16[4,192,768]{2,1,0:T(8,128)(2,1)}), bf16[4,192,768]{2,1,0:T(8,128)(2,1)}, u32[]{:S(2)}, u32[]{:S(2)}) async-start(bf16[4,192,768]{2,1,0:T(8,128)(2,1)} %broadcast_in_dim.34), calls=%async_computation.4 | async-start | bytes 2359296 | tf_op jit(solution)/shard_map/all_to_all | solution.py:89
  231.6 28.0 %all-to-all-start.4 = ((bf16[128,8,288]{0,2,1:T(8,128)(2,1)}), bf16[128,8,288]{0,2,1:T(8,128)(2,1)}, u32[]{:S(2)}, u32[]{:S(2)}) async-start(bf16[128,8,288]{0,2,1:T(8,128)(2,1)} %bitcast.105), calls=%async_computation.5 | async-start | bytes 1179648 | tf_op jit(solution)/shard_map/all_to_all | solution.py:89
  259.6 24.1 %all-to-all-start.7 = ((bf16[128,8,96]{0,2,1:T(8,128)(2,1)}), bf16[128,8,96]{0,2,1:T(8,128)(2,1)}, u32[]{:S(2)}, u32[]{:S(2)}) async-start(bf16[128,8,96]{0,2,1:T(8,128)(2,1)} %bitcast.107), calls=%async_computation.9 | async-start | bytes 393216 | tf_op jit(solution)/shard_map/all_to_all | solution.py:89
  263.8 79.9 %reduce-scatter.5.cloned.1.call-start = ((), (), s32[]{:S(2)}) async-start(), calls=%async_computation.17 | async-start | bytes 1769472 | tf_op jit(solution)/shard_map/reduce_scatter | solution.py:215
  283.7 10.9 %all-to-all-start.5 = ((f32[8,1,768]{2,1,0:T(1,128)}), f32[8,1,768]{2,1,0:T(1,128)S(1)}, u32[]{:S(2)}, u32[]{:S(2)}) async-start(f32[8,1,768]{2,1,0:T(1,128)} %all_to_all.113), calls=%async_computation.7 | async-start | bytes 49152 | tf_op jit(solution)/shard_map/all_to_all | solution.py:89
  294.6 13.4 %all-to-all-start.8 = ((bf16[4,96,768]{2,1,0:T(8,128)(2,1)}), bf16[4,96,768]{2,1,0:T(8,128)(2,1)}, u32[]{:S(2)}, u32[]{:S(2)}) async-start(bf16[4,96,768]{2,1,0:T(8,128)(2,1)} %pad_maximum_fusion.2), calls=%async_computation.10 | async-start | bytes 1179648 | tf_op jit(solution)/shard_map/all_to_all | solution.py:89
  308.7 7.9 %all-to-all-start.6 = ((f32[4,1,1152]{2,1,0:T(1,128)}), f32[4,1,1152]{2,1,0:T(1,128)S(1)}, u32[]{:S(2)}, u32[]{:S(2)}) async-start(f32[4,1,1152]{2,1,0:T(1,128)} %broadcast_in_dim.37), calls=%async_computation.8 | async-start | bytes 36864 | tf_op jit(solution)/shard_map/all_to_all | solution.py:89
  316.6 11.0 %all-to-all-start.9 = ((bf16[8,24,288]{2,1,0:T(8,128)(2,1)}), bf16[8,24,288]{2,1,0:T(8,128)(2,1)}, u32[]{:S(2)}, u32[]{:S(2)}) async-start(bf16[8,24,288]{2,1,0:T(8,128)(2,1)} %all_to_all.109), calls=%async_computation.11 | async-start | bytes 294912 | tf_op jit(solution)/shard_map/all_to_all | solution.py:89
  329.7 12.0 %all-to-all-start.10 = ((bf16[4,96,768]{2,1,0:T(8,128)(2,1)}), bf16[4,96,768]{2,1,0:T(8,128)(2,1)S(1)}, u32[]{:S(2)}, u32[]{:S(2)}) async-start(bf16[4,96,768]{2,1,0:T(8,128)(2,1)} %broadcast_in_dim.68), calls=%async_computation.12 | async-start | bytes 1179648 | tf_op jit(solution)/shard_map/all_to_all | solution.py:89
  (38 other events, 699.6 us)
Sparse Core Ops, SparseCore 0:
  9.7 49.0 all-gather.6
  90.9 23.5 all-gather.8
  116.1 33.6 all-gather.10
  162.0 33.8 reduce-scatter.2
  197.3 25.0 all-gather.14
  224.5 29.5 all-gather.12
  266.9 35.7 reduce-scatter.4
